TPU v7x, 256 devices: a whole 4x4x8 slice. The times are simulated.
256 devices in a mesh: dp: 2 (over core), blk: 128 (over z, x, y).
Axes of the slice: x: 4, y: 4, z: 8, core: 2. Of those that a mesh axis runs over, the one named last changes fastest.
Arguments:
- features: bfloat16 [2, 65536, 128], P('dp', 'blk'), may hold values from -24 to 24
- tile_mask: int32 [2, 128], P('dp', 'blk'), may hold values 0 or 1
- w_first: bfloat16 [3456, 128], replicated, may hold values from -0.109375 to 0.109375
- w_second: bfloat16 [3456, 128], replicated, may hold values from -0.109375 to 0.109375
- cotangent: bfloat16 [2, 65536, 128], P('dp', 'blk'), may hold values from -6 to 6
Outputs:
- grad_first: float32 [3456, 128], replicated
- grad_second: float32 [3456, 128], replicated
- feature_grad: bfloat16 [2, 65536, 128], P('dp', 'blk')
All inputs are finite; a program needn't handle non-finite values. No bound on the sum of `tile_mask` on one device may be relied on, other than what follows from the above.
Results may differ from a plain program's by a relative error of at most 0.0039.
Values may be sent and summed in bfloat16 or wider, within the bound.
A program may use at most 64 MiB of HBM per device.

v0:
```python
import jax
import jax.numpy as jnp
from jax import lax
from jax.sharding import PartitionSpec as P

TILE = 8
unscale = 1.0 / 512.0


def shifted(value, axis, steps):
    count = lax.axis_size(axis)
    leading, last = (max(0, -steps), min(count, count - steps))
    return lax.ppermute(value, axis, [(source, source + steps) for source in range(leading, last)])


def stack_depth(padded, depth_z):
    return jnp.concatenate(
        [padded[:, :, shift_z : shift_z + depth_z, :] for shift_z in range(3)], axis=-1
    )


def arrange(weight):
    width_in = weight.shape[0] // 27
    width_out = weight.shape[1]
    shaped = weight.reshape(width_in, 3, 3, 3, width_out).transpose(1, 2, 3, 0, 4)
    return shaped.reshape(3, 3, 3 * width_in, width_out)


def arrange_flipped(weight):
    width_in = weight.shape[0] // 27
    width_out = weight.shape[1]
    shaped = weight.reshape(width_in, 3, 3, 3, width_out)[:, ::-1, ::-1, ::-1, :].transpose(
        1, 2, 3, 4, 0
    )
    return shaped.reshape(3, 3, 3 * width_out, width_in)


def convolve(padded, kernel):
    size_x = padded.shape[0] - 2
    size_y = padded.shape[1] - 2
    size_z = padded.shape[2] - 2
    stacked = stack_depth(padded, size_z)
    summed = jnp.zeros((size_x * size_y * size_z, kernel.shape[-1]), jnp.float32)
    for step_x in range(3):
        for step_y in range(3):
            slab_rows = stacked[step_x : step_x + size_x, step_y : step_y + size_y].reshape(
                -1, stacked.shape[-1]
            )
            summed = summed + jnp.dot(
                slab_rows, kernel[step_x, step_y], preferred_element_type=jnp.float32
            )
    return summed


def correlate(padded, grads):
    size_x = padded.shape[0] - 2
    size_y = padded.shape[1] - 2
    size_z = padded.shape[2] - 2
    width_in = padded.shape[3]
    width_out = grads.shape[1]
    stacked = stack_depth(padded, size_z)
    blocks = []
    for step_x in range(3):
        for step_y in range(3):
            slab_rows = stacked[step_x : step_x + size_x, step_y : step_y + size_y].reshape(
                -1, stacked.shape[-1]
            )
            blocks.append(
                lax.dot_general(
                    slab_rows, grads, (((0,), (0,)), ((), ())), preferred_element_type=jnp.float32
                )
            )
    joined = jnp.stack(blocks).reshape(3, 3, 3, width_in, width_out).transpose(3, 0, 1, 2, 4)
    return joined.reshape(27 * width_in, width_out)


def direct_rims(values, place, extent):
    padded = jnp.pad(values, ((1, 1), (1, 1), (1, 1), (0, 0)))
    for shift_x in (-1, 0, 1):
        for shift_y in (-1, 0, 1):
            for shift_z in (-1, 0, 1):
                moves = (shift_x, shift_y, shift_z)
                if moves == (0, 0, 0):
                    continue
                sliced = values
                inside = jnp.asarray(True)
                starts = []
                for axis_pos in range(3):
                    toward = moves[axis_pos]
                    length = values.shape[axis_pos]
                    if toward == 1:
                        sliced = lax.slice_in_dim(sliced, 0, 1, axis=axis_pos)
                        starts.append(length + 1)
                    elif toward == -1:
                        sliced = lax.slice_in_dim(sliced, length - 1, length, axis=axis_pos)
                        starts.append(0)
                    else:
                        starts.append(1)
                    inside = (
                        inside
                        & (place[axis_pos] + toward >= 0)
                        & (place[axis_pos] + toward < extent[axis_pos])
                    )
                offset = shift_x * 16 + shift_y * 4 + shift_z
                arrived = shifted(sliced, "blk", -offset)
                arrived = jnp.where(inside, arrived, jnp.zeros_like(arrived))
                padded = lax.dynamic_update_slice(
                    padded, arrived, (starts[0], starts[1], starts[2], 0)
                )
    return padded


def surround(values, place, extent):
    return direct_rims(values, place, extent)


def reduce_rows(term):
    return lax.psum(term, ("dp", "blk"))


def on_device(features, tile_mask, w_first, w_second, cotangent):
    width = features.shape[2]
    size_x = tile_mask.shape[1] * TILE
    region = (size_x, TILE, TILE, width)
    device_index = lax.axis_index("blk")
    place = (device_index // 16, device_index // 4 % 4, device_index % 4)
    extent = (lax.axis_size("blk") // 16, 4, 4)
    keep_rows = jnp.repeat(tile_mask[0], TILE * TILE * TILE).astype(jnp.bfloat16)[:, None]
    keep_float = keep_rows.astype(jnp.float32)
    inputs = features[0] * keep_rows
    grads_out = cotangent[0] * keep_rows
    pad_in = surround(inputs.reshape(region), place, extent)
    pre_act = convolve(pad_in, arrange(w_first))
    hidden = (jax.nn.silu(pre_act) * keep_float).astype(jnp.bfloat16)
    pad_hidden = surround(hidden.reshape(region), place, extent)
    pad_grads = surround(grads_out.reshape(region), place, extent)
    grad_second = reduce_rows(correlate(pad_hidden, grads_out) * unscale)
    back = convolve(pad_grads, arrange_flipped(w_second))
    sigma = jax.nn.sigmoid(pre_act)
    pre_grad = (back * sigma * (1.0 + pre_act * (1.0 - sigma)) * keep_float).astype(jnp.bfloat16)
    pad_pre = surround(pre_grad.reshape(region), place, extent)
    grad_first = reduce_rows(correlate(pad_in, pre_grad) * unscale)
    summed = grads_out.astype(jnp.float32) + convolve(pad_pre, arrange_flipped(w_first))
    result = (summed * keep_float).astype(jnp.bfloat16)
    return (grad_first, grad_second, result[None])


def solution(mesh):
    in_specs = (P("dp", "blk", None), P("dp", "blk"), P(), P(), P("dp", "blk", None))
    out_specs = (P(), P(), P("dp", "blk", None))
    return jax.shard_map(
        on_device, mesh=mesh, in_specs=in_specs, out_specs=out_specs, check_vma=False
    )
```

profile of v0, /device:TPU:97, one launch (start us, length us, event | category | flops | bytes accessed | tf_op | source)
XLA Modules:
  0.0 1220.6 jit_solution(1918076127340199430)
XLA Ops:
  14.3 7.1 collective-permute-start.8
  71.6 9.0 collective-permute-start.2
  81.3 6.9 collective-permute-start.28
  91.5 7.8 collective-permute-done
  101.2 7.8 collective-permute-done.26
  110.9 5.4 collective-permute-done.25
  126.1 7.2 collective-permute-done.23
  135.2 5.7 collective-permute-done.49
  150.0 5.4 collective-permute-done.45
  159.1 8.3 collective-permute-done.17
  169.4 6.0 collective-permute-done.43
  180.6 5.5 collective-permute-start.16
  218.5 6.1 collective-permute-done.35
  227.1 6.3 collective-permute-done.9
  233.5 8.0 collective-permute-start.5
  242.2 6.9 collective-permute-start.31
  249.9 8.9 collective-permute-start.3
  259.5 5.7 collective-permute-start.29
  284.4 12.4 %collective-permute-done.20 = bf16[1,8,1,128]{3,2,1,0:T(2,128)(2,1)S(1)} collective-permute-done((bf16[1,8,1,128]{3,2,1,0:T(2,128)(2,1)S(1)}, bf16[1,8,1,128]{3,2,1,0:T(2,128)(2,1)S(1)}, u32[]{:S(2)}, u32[]{:S(2)}) %collective-permute-start.20) | collective-permute-done | bytes 2080 | tf_op jit(solution)/shard_map/ppermute | solution.py:13
  298.7 5.7 collective-permute-done.46
  324.4 5.4 collective-permute-done.27
  362.0 7.0 collective-permute-done.12
  400.1 6.3 collective-permute-done.38
  452.5 9.4 collective-permute-start.82
  490.7 6.3 collective-permute-done.80
  501.0 5.8 collective-permute-done.78
  508.6 5.4 collective-permute-done.103
  516.0 5.9 collective-permute-done.101
  530.5 6.2 collective-permute-done.95
  549.4 6.2 collective-permute-start.54
  560.0 7.6 collective-permute-done.52
  569.6 5.4 collective-permute-done.77
  576.9 5.9 collective-permute-done.75
  591.8 5.5 collective-permute-done.69
  597.2 5.9 collective-permute-start.68
  619.5 6.5 collective-permute-done.61
  647.1 6.7 collective-permute-done.87
  653.8 8.9 collective-permute-start.83
  681.7 6.2 collective-permute-done.98
  687.9 5.5 collective-permute-start.57
  696.2 7.7 collective-permute-done.55
  712.5 6.2 collective-permute-done.72
  726.1 5.7 collective-permute-done.79
  749.7 8.7 collective-permute-start.53
  771.9 6.7 collective-permute-start.65
  781.6 7.2 collective-permute-done.64
  816.7 7.0 collective-permute-done.90
  840.7 368.9 %all-reduce.7.cloned.1.call-done = (f32[3456,128]{1,0:T(8,128)}, f32[3456,128]{1,0:T(8,128)}) async-done(((f32[3456,128]{1,0:T(8,128)}, f32[3456,128]{1,0:T(8,128)}), (f32[3456,128]{1,0:T(8,128)}, f32[3456,128]{1,0:T(8,128)})) %all-reduce.7.cloned.1.call-update) | async-done | bytes 3538960 | tf_op jit(solution)/shard_map/psum | solution.py:118
  (610 shorter events, 514.2 us)
Async XLA Ops:
  7.2 1202.4 %all-reduce.7.cloned.1.call-start = ((), (), s32[]{:S(2)}) async-start(), calls=%async_computation | async-start | bytes 7077888 | tf_op jit(solution)/shard_map/psum | solution.py:118
  8.9 376.5 %collective-permute-start.4 = (bf16[1,8,8,128]{3,2,1,0:T(8,128)(2,1)S(1)}, bf16[1,8,8,128]{3,2,1,0:T(8,128)(2,1)S(1)}, u32[]{:S(2)}, u32[]{:S(2)}) collective-permute-start(bf16[1,8,8,128]{3,2,1,0:T(8,128)(2,1)S(1)} %get-tuple-element.84), channel_id=1, source_target_pairs={{0,16},{1,17},{2,18},{3,19},{4,20},{5,21},{6,22},{7,23},{8,24},{9,... | collective-permute-start | bytes 49160 | tf_op jit(solution)/shard_map/ppermute | solution.py:13
  14.3 38.4 %collective-permute-start.8 = (bf16[1,1,1,128]{3,2,1,0:T(2,128)(2,1)}, bf16[1,1,1,128]{3,2,1,0:T(2,128)(2,1)}, u32[]{:S(2)}, u32[]{:S(2)}) collective-permute-start(bf16[1,1,1,128]{3,2,1,0:T(2,128)(2,1)} %get-tuple-element.149), channel_id=1, source_target_pairs={{0,11},{1,12},{2,13},{3,14},{4,15},{5,16},{6,17},{7,18},{8,19},{9,... | collective-permute-start | bytes 776 | tf_op jit(solution)/shard_map/ppermute | solution.py:13
  21.4 367.4 %collective-permute-start.21 = (bf16[1,8,8,128]{3,2,1,0:T(8,128)(2,1)S(1)}, bf16[1,8,8,128]{3,2,1,0:T(8,128)(2,1)S(1)}, u32[]{:S(2)}, u32[]{:S(2)}) collective-permute-start(bf16[1,8,8,128]{3,2,1,0:T(8,128)(2,1)S(1)} %get-tuple-element.83), channel_id=1, source_target_pairs={{16,0},{17,1},{18,2},{19,3},{20,4},{21,5},{22,6},{23,7},{24,8},{25... | collective-permute-start | bytes 49160 | tf_op jit(solution)/shard_map/ppermute | solution.py:13
  23.4 408.3 %collective-permute-start.47 = (bf16[1,8,8,128]{3,2,1,0:T(8,128)(2,1)S(1)}, bf16[1,8,8,128]{3,2,1,0:T(8,128)(2,1)S(1)}, u32[]{:S(2)}, u32[]{:S(2)}) collective-permute-start(bf16[1,8,8,128]{3,2,1,0:T(8,128)(2,1)S(1)} %get-tuple-element.73), channel_id=1, source_target_pairs={{16,0},{17,1},{18,2},{19,3},{20,4},{21,5},{22,6},{23,7},{24,8},{25... | collective-permute-start | bytes 49160 | tf_op jit(solution)/shard_map/ppermute | solution.py:13
  25.3 382.5 %collective-permute-start.30 = (bf16[1,8,8,128]{3,2,1,0:T(8,128)(2,1)S(1)}, bf16[1,8,8,128]{3,2,1,0:T(8,128)(2,1)}, u32[]{:S(2)}, u32[]{:S(2)}) collective-permute-start(bf16[1,8,8,128]{3,2,1,0:T(8,128)(2,1)S(1)} %get-tuple-element.74), channel_id=1, source_target_pairs={{0,16},{1,17},{2,18},{3,19},{4,20},{5,21},{6,22},{7,23},{8,24},{9,... | collective-permute-start | bytes 49160 | tf_op jit(solution)/shard_map/ppermute | solution.py:13
  71.6 9.7 collective-permute-start.2
  81.3 8.2 collective-permute-start.28
  89.5 9.7 collective-permute-start
  99.3 9.7 collective-permute-start.26
  123.6 9.7 collective-permute-start.23
  155.4 12.0 collective-permute-start.17
  167.4 7.9 collective-permute-start.43
  186.9 8.6 collective-permute-start.40
  215.7 8.9 collective-permute-start.35
  224.6 8.9 collective-permute-start.9
  233.5 8.7 collective-permute-start.5
  249.9 9.6 collective-permute-start.3
  259.5 9.5 collective-permute-start.29
  281.9 14.9 %collective-permute-start.20 = (bf16[1,8,1,128]{3,2,1,0:T(2,128)(2,1)S(1)}, bf16[1,8,1,128]{3,2,1,0:T(2,128)(2,1)S(1)}, u32[]{:S(2)}, u32[]{:S(2)}) collective-permute-start(bf16[1,8,1,128]{3,2,1,0:T(2,128)(2,1)S(1)} %get-tuple-element.148), channel_id=1, source_target_pairs={{15,0},{16,1},{17,2},{18,3},{19,4},{20,5},{21,6},{22,7},{23,8},{24... | collective-permute-start | bytes 6152 | tf_op jit(solution)/shard_map/ppermute | solution.py:13
  360.0 9.0 collective-permute-start.12
  382.0 25.0 %collective-permute-start.41 = (bf16[8,1,8,128]{3,2,1,0:T(8,128)(2,1)}, bf16[8,1,8,128]{3,2,1,0:T(8,128)(2,1)}, u32[]{:S(2)}, u32[]{:S(2)}) collective-permute-start(bf16[8,1,8,128]{3,2,1,0:T(8,128)(2,1)} %get-tuple-element.79), channel_id=1, source_target_pairs={{4,0},{5,1},{6,2},{7,3},{8,4},{9,5},{10,6},{11,7},{12,8},{13,9},{1... | collective-permute-start | bytes 49160 | tf_op jit(solution)/shard_map/ppermute | solution.py:13
  385.4 22.4 %collective-permute-start.36 = (bf16[8,1,8,128]{3,2,1,0:T(8,128)(2,1)}, bf16[8,1,8,128]{3,2,1,0:T(8,128)(2,1)}, u32[]{:S(2)}, u32[]{:S(2)}) collective-permute-start(bf16[8,1,8,128]{3,2,1,0:T(8,128)(2,1)} %get-tuple-element.80), channel_id=1, source_target_pairs={{0,4},{1,5},{2,6},{3,7},{4,8},{5,9},{6,10},{7,11},{8,12},{9,13},{1... | collective-permute-start | bytes 49160 | tf_op jit(solution)/shard_map/ppermute | solution.py:13
  388.8 8.5 collective-permute-start.39
  397.3 9.1 collective-permute-start.38
  448.3 377.5 %collective-permute-start.99 = (bf16[1,8,8,128]{3,2,1,0:T(8,128)(2,1)S(1)}, bf16[1,8,8,128]{3,2,1,0:T(8,128)(2,1)S(1)}, u32[]{:S(2)}, u32[]{:S(2)}) collective-permute-start(bf16[1,8,8,128]{3,2,1,0:T(8,128)(2,1)S(1)} %get-tuple-element.53), channel_id=1, source_target_pairs={{16,0},{17,1},{18,2},{19,3},{20,4},{21,5},{22,6},{23,7},{24,8},{25... | collective-permute-start | bytes 49160 | tf_op jit(solution)/shard_map/ppermute | solution.py:13
  452.5 371.2 %collective-permute-start.82 = (bf16[1,8,8,128]{3,2,1,0:T(8,128)(2,1)S(1)}, bf16[1,8,8,128]{3,2,1,0:T(8,128)(2,1)}, u32[]{:S(2)}, u32[]{:S(2)}) collective-permute-start(bf16[1,8,8,128]{3,2,1,0:T(8,128)(2,1)S(1)} %get-tuple-element.54), channel_id=1, source_target_pairs={{0,16},{1,17},{2,18},{3,19},{4,20},{5,21},{6,22},{7,23},{8,24},{9,... | collective-permute-start | bytes 49160 | tf_op jit(solution)/shard_map/ppermute | solution.py:13
  465.5 343.6 %collective-permute-start.73 = (bf16[1,8,8,128]{3,2,1,0:T(8,128)(2,1)S(1)}, bf16[1,8,8,128]{3,2,1,0:T(8,128)(2,1)}, u32[]{:S(2)}, u32[]{:S(2)}) collective-permute-start(bf16[1,8,8,128]{3,2,1,0:T(8,128)(2,1)S(1)} %get-tuple-element.63), channel_id=1, source_target_pairs={{16,0},{17,1},{18,2},{19,3},{20,4},{21,5},{22,6},{23,7},{24,8},{25... | collective-permute-start | bytes 49160 | tf_op jit(solution)/shard_map/ppermute | solution.py:13
  467.4 337.4 %collective-permute-start.56 = (bf16[1,8,8,128]{3,2,1,0:T(8,128)(2,1)S(1)}, bf16[1,8,8,128]{3,2,1,0:T(8,128)(2,1)}, u32[]{:S(2)}, u32[]{:S(2)}) collective-permute-start(bf16[1,8,8,128]{3,2,1,0:T(8,128)(2,1)S(1)} %get-tuple-element.64), channel_id=1, source_target_pairs={{0,16},{1,17},{2,18},{3,19},{4,20},{5,21},{6,22},{7,23},{8,24},{9,... | collective-permute-start | bytes 49160 | tf_op jit(solution)/shard_map/ppermute | solution.py:13
  473.8 8.3 collective-permute-start.86
  488.7 8.3 collective-permute-start.80
  497.0 9.7 collective-permute-start.78
  528.5 8.1 collective-permute-start.95
  549.4 8.3 collective-permute-start.54
  557.7 9.9 collective-permute-start.52
  589.3 7.9 collective-permute-start.69
  617.2 8.9 collective-permute-start.61
  644.8 9.1 collective-permute-start.87
  653.8 9.6 collective-permute-start.83
  663.4 9.7 collective-permute-start.81
  679.7 8.1 collective-permute-start.98
  694.3 9.7 collective-permute-start.55
  710.6 8.2 collective-permute-start.72
  749.7 9.6 collective-permute-start.53
  779.7 9.2 collective-permute-start.64
  801.4 22.2 %collective-permute-start.93 = (bf16[8,1,8,128]{3,2,1,0:T(8,128)(2,1)}, bf16[8,1,8,128]{3,2,1,0:T(8,128)(2,1)S(1)}, u32[]{:S(2)}, u32[]{:S(2)}) collective-permute-start(bf16[8,1,8,128]{3,2,1,0:T(8,128)(2,1)} %get-tuple-element.59), channel_id=1, source_target_pairs={{4,0},{5,1},{6,2},{7,3},{8,4},{9,5},{10,6},{11,7},{12,8},{13,9},{1... | collective-permute-start | bytes 49160 | tf_op jit(solution)/shard_map/ppermute | solution.py:13
  804.8 18.9 %collective-permute-start.88 = (bf16[8,1,8,128]{3,2,1,0:T(8,128)(2,1)}, bf16[8,1,8,128]{3,2,1,0:T(8,128)(2,1)S(1)}, u32[]{:S(2)}, u32[]{:S(2)}) collective-permute-start(bf16[8,1,8,128]{3,2,1,0:T(8,128)(2,1)} %get-tuple-element.60), channel_id=1, source_target_pairs={{0,4},{1,5},{2,6},{3,7},{4,8},{5,9},{6,10},{7,11},{8,12},{9,13},{1... | collective-permute-start | bytes 49160 | tf_op jit(solution)/shard_map/ppermute | solution.py:13
  814.7 8.9 collective-permute-start.90
  (118 other events, 7307.3 us)
Sparse Core Ops, SparseCore 0:
  836.7 372.8 all-reduce.6
where the time goes:
time: 1230 us; the launch traced here: 1220 us
  waiting for transfers between devices  736 us (60%)
  starting transfers between devices  346 us (28%)
  local copies, waits for them, and re-layouts  88.6 us (7%)
  between operations  18 us (1%)
  other arithmetic  16.7 us (1%)
  matrix products  15.1 us (1%)
    psum x1, waiting for transfers between devices, reduce_rows(): return lax.psum(term, ('dp', 'blk'))  369 us
    ppermute x104, waiting for transfers between devices, shifted(): lax.ppermute(value, axis, [(source, source + steps) for source in range(l...  367 us
    ppermute x104, starting transfers between devices, shifted(): lax.ppermute(value, axis, [(source, source + steps) for source in range(l...  346 us
    dynamic_update_slice x104, local copies, waits for them, and re-layouts, direct_rims(): lax.dynamic_update_slice(padded, arrived, (starts[0], starts[1], starts[2...  35.9 us
  transfers between devices with their start and end apart: 105, of which 89 were waited for; matrix products, arithmetic and copies ran while one was open for 7% of the time, Pallas kernels for 0%

commit v1 on v0

--- a/solution.py
+++ b/solution.py
@@ -5,6 +5,12 @@
 
 TILE = 8
 unscale = 1.0 / 512.0
+
+
+def cover_the_members_all(own_rows, device_axis, axis_tag):
+    for j0 in (device_axis, axis_tag):
+        own_rows = lax.psum(own_rows, j0)
+    return own_rows
 
 
 def shifted(value, axis, steps):
@@ -115,7 +121,7 @@
 
 
 def reduce_rows(term):
-    return lax.psum(term, ("dp", "blk"))
+    return cover_the_members_all(term, "blk", "dp")
 
 
 def on_device(features, tile_mask, w_first, w_second, cotangent):

time: 1230 us -> 1090 us (0.89)
  waiting for transfers between devices: 736 us -> 602 us
    psum x1 -> x2, waiting for transfers between devices: 369 us -> 253 us  [cover_the_members_all(): own_rows = lax.psum(own_rows, j0)]
    ppermute x104, waiting for transfers between devices: 367 us -> 350 us  [shifted(): lax.ppermute(value, axis, [(source, source + steps) for source in range(l...]
  transfers between devices with their start and end apart: 105 -> 106, of which waited for: 89 -> 86; matrix products, arithmetic and copies ran while one was open for 7% -> 9% of each run, Pallas kernels for 0% -> 0%
where the time goes in v1:
time: 1090 us; the launch traced here: 1080 us
  waiting for transfers between devices  602 us (55%)
  starting transfers between devices  344 us (32%)
  local copies, waits for them, and re-layouts  87.4 us (8%)
  between operations  18 us (2%)
  other arithmetic  16.6 us (2%)
  matrix products  14.2 us (1%)
    ppermute x104, waiting for transfers between devices, shifted(): lax.ppermute(value, axis, [(source, source + steps) for source in range(l...  350 us
    ppermute x104, starting transfers between devices, shifted(): lax.ppermute(value, axis, [(source, source + steps) for source in range(l...  344 us
    psum x2, waiting for transfers between devices, cover_the_members_all(): own_rows = lax.psum(own_rows, j0)  253 us
    dynamic_update_slice x104, local copies, waits for them, and re-layouts, direct_rims(): lax.dynamic_update_slice(padded, arrived, (starts[0], starts[1], starts[2...  36 us
  transfers between devices with their start and end apart: 106, of which 86 were waited for; matrix products, arithmetic and copies ran while one was open for 9% of the time, Pallas kernels for 0%

profile of v1, /device:TPU:97, one launch (start us, length us, event | category | flops | bytes accessed | tf_op | source)
XLA Modules:
  0.0 1082.4 jit_solution(9512443539582717492)
XLA Ops:
  14.3 7.1 collective-permute-start.8
  71.7 9.0 collective-permute-start.2
  81.4 6.9 collective-permute-start.28
  91.5 7.8 collective-permute-done
  101.2 7.8 collective-permute-done.26
  110.9 5.4 collective-permute-done.25
  126.1 7.2 collective-permute-done.23
  135.3 5.7 collective-permute-done.49
  150.1 5.4 collective-permute-done.45
  159.2 8.3 collective-permute-done.17
  169.4 6.0 collective-permute-done.43
  180.6 5.5 collective-permute-start.16
  218.5 6.1 collective-permute-done.35
  227.1 6.3 collective-permute-done.9
  233.5 8.0 collective-permute-start.5
  242.2 6.9 collective-permute-start.31
  249.9 8.9 collective-permute-start.3
  259.5 5.7 collective-permute-start.29
  284.4 12.4 %collective-permute-done.20 = bf16[1,8,1,128]{3,2,1,0:T(2,128)(2,1)S(1)} collective-permute-done((bf16[1,8,1,128]{3,2,1,0:T(2,128)(2,1)S(1)}, bf16[1,8,1,128]{3,2,1,0:T(2,128)(2,1)S(1)}, u32[]{:S(2)}, u32[]{:S(2)}) %collective-permute-start.20) | collective-permute-done | bytes 2080 | tf_op jit(solution)/shard_map/ppermute | solution.py:19
  298.7 5.7 collective-permute-done.46
  324.5 5.4 collective-permute-done.27
  362.0 7.0 collective-permute-done.12
  400.1 6.3 collective-permute-done.38
  452.7 9.4 collective-permute-start.82
  490.9 6.3 collective-permute-done.80
  501.2 5.8 collective-permute-done.78
  508.9 5.6 collective-permute-done.103
  516.5 5.7 collective-permute-done.101
  534.9 6.5 collective-permute-start.54
  545.1 8.0 collective-permute-done.52
  555.1 5.4 collective-permute-done.77
  562.4 6.3 collective-permute-done.75
  577.6 5.7 collective-permute-done.69
  583.3 5.6 collective-permute-start.68
  605.6 6.2 collective-permute-done.61
  617.5 8.1 collective-permute-start.55
  635.6 7.1 collective-permute-done.72
  668.3 6.9 collective-permute-start.65
  678.2 7.2 collective-permute-done.64
  718.8 5.7 collective-permute-done.95
  726.5 6.1 collective-permute-start.87
  738.0 10.2 collective-permute-start.83
  750.9 7.5 collective-permute-done.81
  766.8 6.0 collective-permute-done.98
  779.9 5.4 collective-permute-done.79
  804.3 7.2 collective-permute-done.90
  811.5 218.5 %all-reduce.9.cloned.1.call-done = (f32[3456,128]{1,0:T(8,128)}, f32[3456,128]{1,0:T(8,128)}) async-done(((f32[3456,128]{1,0:T(8,128)}, f32[3456,128]{1,0:T(8,128)}), (f32[3456,128]{1,0:T(8,128)}, f32[3456,128]{1,0:T(8,128)})) %all-reduce.9.cloned.1.call-update) | async-done | bytes 3538960 | tf_op jit(solution)/shard_map/psum | solution.py:12
  1037.2 34.3 %all-reduce.11.cloned.1.call-done = (f32[3456,128]{1,0:T(8,128)}, f32[3456,128]{1,0:T(8,128)}) async-done(((f32[3456,128]{1,0:T(8,128)}, f32[3456,128]{1,0:T(8,128)}), (f32[3456,128]{1,0:T(8,128)}, f32[3456,128]{1,0:T(8,128)})) %all-reduce.11.cloned.1.call-update) | async-done | bytes 3538960 | tf_op jit(solution)/shard_map/psum | solution.py:12
  (623 shorter events, 496.7 us)
Async XLA Ops:
  7.2 1022.9 %all-reduce.9.cloned.1.call-start = ((), (), s32[]{:S(2)}) async-start(), calls=%async_computation | async-start | bytes 7077888 | tf_op jit(solution)/shard_map/psum | solution.py:12
  8.9 376.5 %collective-permute-start.4 = (bf16[1,8,8,128]{3,2,1,0:T(8,128)(2,1)S(1)}, bf16[1,8,8,128]{3,2,1,0:T(8,128)(2,1)S(1)}, u32[]{:S(2)}, u32[]{:S(2)}) collective-permute-start(bf16[1,8,8,128]{3,2,1,0:T(8,128)(2,1)S(1)} %get-tuple-element.86), channel_id=1, source_target_pairs={{0,16},{1,17},{2,18},{3,19},{4,20},{5,21},{6,22},{7,23},{8,24},{9,... | collective-permute-start | bytes 49160 | tf_op jit(solution)/shard_map/ppermute | solution.py:19
  14.3 38.4 %collective-permute-start.8 = (bf16[1,1,1,128]{3,2,1,0:T(2,128)(2,1)}, bf16[1,1,1,128]{3,2,1,0:T(2,128)(2,1)}, u32[]{:S(2)}, u32[]{:S(2)}) collective-permute-start(bf16[1,1,1,128]{3,2,1,0:T(2,128)(2,1)} %get-tuple-element.151), channel_id=1, source_target_pairs={{0,11},{1,12},{2,13},{3,14},{4,15},{5,16},{6,17},{7,18},{8,19},{9,... | collective-permute-start | bytes 776 | tf_op jit(solution)/shard_map/ppermute | solution.py:19
  21.4 367.4 %collective-permute-start.21 = (bf16[1,8,8,128]{3,2,1,0:T(8,128)(2,1)S(1)}, bf16[1,8,8,128]{3,2,1,0:T(8,128)(2,1)S(1)}, u32[]{:S(2)}, u32[]{:S(2)}) collective-permute-start(bf16[1,8,8,128]{3,2,1,0:T(8,128)(2,1)S(1)} %get-tuple-element.85), channel_id=1, source_target_pairs={{16,0},{17,1},{18,2},{19,3},{20,4},{21,5},{22,6},{23,7},{24,8},{25... | collective-permute-start | bytes 49160 | tf_op jit(solution)/shard_map/ppermute | solution.py:19
  23.3 408.5 %collective-permute-start.47 = (bf16[1,8,8,128]{3,2,1,0:T(8,128)(2,1)S(1)}, bf16[1,8,8,128]{3,2,1,0:T(8,128)(2,1)S(1)}, u32[]{:S(2)}, u32[]{:S(2)}) collective-permute-start(bf16[1,8,8,128]{3,2,1,0:T(8,128)(2,1)S(1)} %get-tuple-element.75), channel_id=1, source_target_pairs={{16,0},{17,1},{18,2},{19,3},{20,4},{21,5},{22,6},{23,7},{24,8},{25... | collective-permute-start | bytes 49160 | tf_op jit(solution)/shard_map/ppermute | solution.py:19
  25.3 382.6 %collective-permute-start.30 = (bf16[1,8,8,128]{3,2,1,0:T(8,128)(2,1)S(1)}, bf16[1,8,8,128]{3,2,1,0:T(8,128)(2,1)}, u32[]{:S(2)}, u32[]{:S(2)}) collective-permute-start(bf16[1,8,8,128]{3,2,1,0:T(8,128)(2,1)S(1)} %get-tuple-element.76), channel_id=1, source_target_pairs={{0,16},{1,17},{2,18},{3,19},{4,20},{5,21},{6,22},{7,23},{8,24},{9,... | collective-permute-start | bytes 49160 | tf_op jit(solution)/shard_map/ppermute | solution.py:19
  71.7 9.7 collective-permute-start.2
  89.6 9.7 collective-permute-start
  99.3 9.7 collective-permute-start.26
  123.6 9.7 collective-permute-start.23
  155.4 12.0 %collective-permute-start.17 = (bf16[1,1,1,128]{3,2,1,0:T(2,128)(2,1)S(1)}, bf16[1,1,1,128]{3,2,1,0:T(2,128)(2,1)S(1)}, u32[]{:S(2)}, u32[]{:S(2)}) collective-permute-start(bf16[1,1,1,128]{3,2,1,0:T(2,128)(2,1)S(1)} %copy-done.51), channel_id=1, source_target_pairs={{11,0},{12,1},{13,2},{14,3},{15,4},{16,5},{17,6},{18,7},{19,8},{20... | collective-permute-start | bytes 776 | tf_op jit(solution)/shard_map/ppermute | solution.py:19
  186.9 8.6 collective-permute-start.40
  215.8 8.9 collective-permute-start.35
  224.6 8.9 collective-permute-start.9
  233.5 8.7 collective-permute-start.5
  249.9 9.6 collective-permute-start.3
  259.5 9.5 collective-permute-start.29
  281.9 14.9 %collective-permute-start.20 = (bf16[1,8,1,128]{3,2,1,0:T(2,128)(2,1)S(1)}, bf16[1,8,1,128]{3,2,1,0:T(2,128)(2,1)S(1)}, u32[]{:S(2)}, u32[]{:S(2)}) collective-permute-start(bf16[1,8,1,128]{3,2,1,0:T(2,128)(2,1)S(1)} %get-tuple-element.150), channel_id=1, source_target_pairs={{15,0},{16,1},{17,2},{18,3},{19,4},{20,5},{21,6},{22,7},{23,8},{24... | collective-permute-start | bytes 6152 | tf_op jit(solution)/shard_map/ppermute | solution.py:19
  360.1 9.0 collective-permute-start.12
  382.1 25.0 %collective-permute-start.41 = (bf16[8,1,8,128]{3,2,1,0:T(8,128)(2,1)}, bf16[8,1,8,128]{3,2,1,0:T(8,128)(2,1)}, u32[]{:S(2)}, u32[]{:S(2)}) collective-permute-start(bf16[8,1,8,128]{3,2,1,0:T(8,128)(2,1)} %get-tuple-element.81), channel_id=1, source_target_pairs={{4,0},{5,1},{6,2},{7,3},{8,4},{9,5},{10,6},{11,7},{12,8},{13,9},{1... | collective-permute-start | bytes 49160 | tf_op jit(solution)/shard_map/ppermute | solution.py:19
  385.4 22.4 %collective-permute-start.36 = (bf16[8,1,8,128]{3,2,1,0:T(8,128)(2,1)}, bf16[8,1,8,128]{3,2,1,0:T(8,128)(2,1)}, u32[]{:S(2)}, u32[]{:S(2)}) collective-permute-start(bf16[8,1,8,128]{3,2,1,0:T(8,128)(2,1)} %get-tuple-element.82), channel_id=1, source_target_pairs={{0,4},{1,5},{2,6},{3,7},{4,8},{5,9},{6,10},{7,11},{8,12},{9,13},{1... | collective-permute-start | bytes 49160 | tf_op jit(solution)/shard_map/ppermute | solution.py:19
  388.8 8.5 collective-permute-start.39
  397.4 9.1 collective-permute-start.38
  448.5 583.8 %collective-permute-start.99 = (bf16[1,8,8,128]{3,2,1,0:T(8,128)(2,1)S(1)}, bf16[1,8,8,128]{3,2,1,0:T(8,128)(2,1)S(1)}, u32[]{:S(2)}, u32[]{:S(2)}) collective-permute-start(bf16[1,8,8,128]{3,2,1,0:T(8,128)(2,1)S(1)} %get-tuple-element.55), channel_id=1, source_target_pairs={{16,0},{17,1},{18,2},{19,3},{20,4},{21,5},{22,6},{23,7},{24,8},{25... | collective-permute-start | bytes 49160 | tf_op jit(solution)/shard_map/ppermute | solution.py:19
  452.7 577.4 %collective-permute-start.82 = (bf16[1,8,8,128]{3,2,1,0:T(8,128)(2,1)S(1)}, bf16[1,8,8,128]{3,2,1,0:T(8,128)(2,1)}, u32[]{:S(2)}, u32[]{:S(2)}) collective-permute-start(bf16[1,8,8,128]{3,2,1,0:T(8,128)(2,1)S(1)} %get-tuple-element.56), channel_id=1, source_target_pairs={{0,16},{1,17},{2,18},{3,19},{4,20},{5,21},{6,22},{7,23},{8,24},{9,... | collective-permute-start | bytes 49160 | tf_op jit(solution)/shard_map/ppermute | solution.py:19
  465.7 238.3 %collective-permute-start.73 = (bf16[1,8,8,128]{3,2,1,0:T(8,128)(2,1)S(1)}, bf16[1,8,8,128]{3,2,1,0:T(8,128)(2,1)}, u32[]{:S(2)}, u32[]{:S(2)}) collective-permute-start(bf16[1,8,8,128]{3,2,1,0:T(8,128)(2,1)S(1)} %get-tuple-element.65), channel_id=1, source_target_pairs={{16,0},{17,1},{18,2},{19,3},{20,4},{21,5},{22,6},{23,7},{24,8},{25... | collective-permute-start | bytes 49160 | tf_op jit(solution)/shard_map/ppermute | solution.py:19
  467.6 232.3 %collective-permute-start.56 = (bf16[1,8,8,128]{3,2,1,0:T(8,128)(2,1)S(1)}, bf16[1,8,8,128]{3,2,1,0:T(8,128)(2,1)}, u32[]{:S(2)}, u32[]{:S(2)}) collective-permute-start(bf16[1,8,8,128]{3,2,1,0:T(8,128)(2,1)S(1)} %get-tuple-element.66), channel_id=1, source_target_pairs={{0,16},{1,17},{2,18},{3,19},{4,20},{5,21},{6,22},{7,23},{8,24},{9,... | collective-permute-start | bytes 49160 | tf_op jit(solution)/shard_map/ppermute | solution.py:19
  474.1 8.3 collective-permute-start.86
  489.0 8.3 collective-permute-start.80
  497.2 9.8 collective-permute-start.78
  534.9 8.3 collective-permute-start.54
  543.2 9.9 collective-permute-start.52
  560.5 8.3 collective-permute-start.75
  603.0 8.9 collective-permute-start.61
  617.5 9.5 collective-permute-start.55
  633.6 9.0 collective-permute-start.72
  676.2 9.2 collective-permute-start.64
  696.8 29.7 %collective-permute-start.94 = (bf16[8,1,1,128]{3,2,1,0:T(2,128)(2,1)}, bf16[8,1,1,128]{3,2,1,0:T(2,128)(2,1)S(1)}, u32[]{:S(2)}, u32[]{:S(2)}) collective-permute-start(bf16[8,1,1,128]{3,2,1,0:T(2,128)(2,1)} %get-tuple-element.57), channel_id=1, source_target_pairs={{5,0},{6,1},{7,2},{8,3},{9,4},{10,5},{11,6},{12,7},{13,8},{14,9},{... | collective-permute-start | bytes 6152 | tf_op jit(solution)/shard_map/ppermute | solution.py:19
  700.0 32.7 %collective-permute-start.92 = (bf16[8,1,1,128]{3,2,1,0:T(2,128)(2,1)}, bf16[8,1,1,128]{3,2,1,0:T(2,128)(2,1)S(1)}, u32[]{:S(2)}, u32[]{:S(2)}) collective-permute-start(bf16[8,1,1,128]{3,2,1,0:T(2,128)(2,1)} %get-tuple-element.58), channel_id=1, source_target_pairs={{3,0},{4,1},{5,2},{6,3},{7,4},{8,5},{9,6},{10,7},{11,8},{12,9},{13... | collective-permute-start | bytes 6152 | tf_op jit(solution)/shard_map/ppermute | solution.py:19
  704.0 12.1 %collective-permute-start.97 = (bf16[1,1,1,128]{3,2,1,0:T(2,128)(2,1)}, bf16[1,1,1,128]{3,2,1,0:T(2,128)(2,1)S(1)}, u32[]{:S(2)}, u32[]{:S(2)}) collective-permute-start(bf16[1,1,1,128]{3,2,1,0:T(2,128)(2,1)} %get-tuple-element.97), channel_id=1, source_target_pairs={{13,0},{14,1},{15,2},{16,3},{17,4},{18,5},{19,6},{20,7},{21,8},{22... | collective-permute-start | bytes 776 | tf_op jit(solution)/shard_map/ppermute | solution.py:19
  716.1 355.3 %all-reduce.11.cloned.1.call-start = ((), (), s32[]{:S(2)}) async-start(), calls=%async_computation.1 | async-start | bytes 7077888 | tf_op jit(solution)/shard_map/psum | solution.py:12
  724.6 11.0 %collective-permute-start.89 = (bf16[8,1,1,128]{3,2,1,0:T(2,128)(2,1)S(1)}, bf16[8,1,1,128]{3,2,1,0:T(2,128)(2,1)S(1)}, u32[]{:S(2)}, u32[]{:S(2)}) collective-permute-start(bf16[8,1,1,128]{3,2,1,0:T(2,128)(2,1)S(1)} %copy-done.25), channel_id=1, source_target_pairs={{0,3},{1,4},{2,5},{3,6},{4,7},{5,8},{6,9},{7,10},{8,11},{9,12},{10... | collective-permute-start | bytes 6152 | tf_op jit(solution)/shard_map/ppermute | solution.py:19
  726.5 11.5 %collective-permute-start.87 = (bf16[8,1,1,128]{3,2,1,0:T(2,128)(2,1)S(1)}, bf16[8,1,1,128]{3,2,1,0:T(2,128)(2,1)S(1)}, u32[]{:S(2)}, u32[]{:S(2)}) collective-permute-start(bf16[8,1,1,128]{3,2,1,0:T(2,128)(2,1)S(1)} %copy-done.24), channel_id=1, source_target_pairs={{0,5},{1,6},{2,7},{3,8},{4,9},{5,10},{6,11},{7,12},{8,13},{9,14},{... | collective-permute-start | bytes 6152 | tf_op jit(solution)/shard_map/ppermute | solution.py:19
  732.7 297.4 %collective-permute-start.93 = (bf16[8,1,8,128]{3,2,1,0:T(8,128)(2,1)S(1)}, bf16[8,1,8,128]{3,2,1,0:T(8,128)(2,1)S(1)}, u32[]{:S(2)}, u32[]{:S(2)}) collective-permute-start(bf16[8,1,8,128]{3,2,1,0:T(8,128)(2,1)S(1)} %copy-done.12), channel_id=1, source_target_pairs={{4,0},{5,1},{6,2},{7,3},{8,4},{9,5},{10,6},{11,7},{12,8},{13,9},{1... | collective-permute-start | bytes 49160 | tf_op jit(solution)/shard_map/ppermute | solution.py:19
  735.6 294.6 %collective-permute-start.88 = (bf16[8,1,8,128]{3,2,1,0:T(8,128)(2,1)S(1)}, bf16[8,1,8,128]{3,2,1,0:T(8,128)(2,1)S(1)}, u32[]{:S(2)}, u32[]{:S(2)}) collective-permute-start(bf16[8,1,8,128]{3,2,1,0:T(8,128)(2,1)S(1)} %copy-done.11), channel_id=1, source_target_pairs={{0,4},{1,5},{2,6},{3,7},{4,8},{5,9},{6,10},{7,11},{8,12},{9,13},{1... | collective-permute-start | bytes 49160 | tf_op jit(solution)/shard_map/ppermute | solution.py:19
  738.0 10.9 %collective-permute-start.83 = (bf16[1,8,1,128]{3,2,1,0:T(2,128)(2,1)S(1)}, bf16[1,8,1,128]{3,2,1,0:T(2,128)(2,1)S(1)}, u32[]{:S(2)}, u32[]{:S(2)}) collective-permute-start(bf16[1,8,1,128]{3,2,1,0:T(2,128)(2,1)S(1)} %copy-done.18), channel_id=1, source_target_pairs={{0,15},{1,16},{2,17},{3,18},{4,19},{5,20},{6,21},{7,22},{8,23},{9,... | collective-permute-start | bytes 6152 | tf_op jit(solution)/shard_map/ppermute | solution.py:19
  748.9 9.5 collective-permute-start.81
  802.3 9.2 collective-permute-start.90
  (124 other events, 7434.2 us)
Sparse Core Ops, SparseCore 0:
  716.2 313.7 all-reduce.8
  1032.7 38.6 all-reduce.10
